TPU v7x, 32 devices: a whole 2x2x4 slice. The times are simulated.
32 devices in a mesh: dp: 8 (over y, x, core), mp: 4 (over z).
Axes of the slice: x: 2, y: 2, z: 4, core: 2. Of those that a mesh axis runs over, the one named last changes fastest.
Arguments:
- act_in: bfloat16 [1024, 4096], P('dp', 'mp'), may hold values from -6 to 6
- grad_in: bfloat16 [1024, 16384], P('dp'), may hold values from -6 to 6
- query_act: bfloat16 [1024, 4096], P('dp', 'mp'), may hold values from -6 to 6
- query_grad: bfloat16 [1024, 16384], P('dp'), may hold values from -6 to 6
- act_basis: bfloat16 [4096, 128], P('mp'), may hold values from -1.1 to 1.1
- grad_basis: bfloat16 [16384, 128], P('dp'), may hold values from -1.1 to 1.1
- seq_lengths: int32 [4], replicated, may hold values from 1 to 256, 768 in all
Outputs:
- moments: float32 [4096, 16384], P('mp', 'dp')
- scores: float32 [64, 4], replicated
Inputs may be any that keep to these rules, and one draw needn't show every extreme that they name: `seq_lengths`: live tokens are the first ones of each sequence, and one sequence is full.
All inputs are finite; a program needn't handle non-finite values.
Results may differ from a plain program's by a relative error of at most 0.0046.
Values may be sent and summed in bfloat16 or wider, within the bound.
A program may use at most 192 MiB of HBM per device.

v0:
```python
import math
import jax
import jax.numpy as jnp
from jax import lax
from jax.sharding import PartitionSpec as P

D = 4096
FF = 16384
QUERIES = 64
QUERY_LEN = 16
damping = 0.1


def rotate(rows_in, basis_rows):
    count_rows, full_width = rows_in.shape
    block_size = basis_rows.shape[1]
    blocks = full_width // block_size
    product = jnp.einsum(
        "nbk,bkc->nbc",
        rows_in.reshape(count_rows, blocks, block_size),
        basis_rows.reshape(blocks, block_size, block_size),
        preferred_element_type=jnp.float32,
    )
    return product.reshape(count_rows, full_width)


def local(act_in, grad_in, query_act, query_grad, act_basis, grad_basis, seq_lengths):
    dp_count = lax.axis_size("dp")
    dp_index = lax.axis_index("dp")
    tok_dev = act_in.shape[0]
    seq_count = seq_lengths.shape[0]
    total_tokens = tok_dev * dp_count
    seq_len = total_tokens // seq_count
    global_rows = dp_index * tok_dev + jnp.arange(tok_dev, dtype=jnp.int32)
    seq_index = global_rows // seq_len
    within = global_rows % seq_len
    matches = seq_index[:, None] == jnp.arange(seq_count, dtype=jnp.int32)[None, :]
    row_length = jnp.sum(jnp.where(matches, seq_lengths[None, :], 0), axis=1)
    live_rows = (within < row_length).astype(jnp.float32)
    act_rot = (rotate(act_in, act_basis) * live_rows[:, None]).astype(jnp.bfloat16)
    query_act_rot = rotate(query_act, act_basis).astype(jnp.bfloat16)
    gathered_act, gathered_query = (
        lax.all_gather(act_rot, "dp", axis=0, tiled=True),
        lax.all_gather(query_act_rot, "dp", axis=0, tiled=True),
    )
    grad_cols, query_cols = (
        lax.all_to_all(grad_in, "dp", split_axis=1, concat_axis=0, tiled=True),
        lax.all_to_all(query_grad, "dp", split_axis=1, concat_axis=0, tiled=True),
    )
    grad_rot = rotate(grad_cols, grad_basis).astype(jnp.bfloat16)
    query_grad_rot = rotate(query_cols, grad_basis).astype(jnp.bfloat16)
    act_square = jnp.square(gathered_act.astype(jnp.float32)).astype(jnp.bfloat16)
    grad_square = jnp.square(grad_rot.astype(jnp.float32)).astype(jnp.bfloat16)
    counted = jnp.sum(seq_lengths).astype(jnp.float32)
    moments = (
        jnp.einsum("ti,tj->ij", act_square, grad_square, preferred_element_type=jnp.float32)
        / counted
    )
    weights = 1.0 / (moments + damping)
    act_width = gathered_act.shape[1]
    grad_width = grad_rot.shape[1]
    seq_acts = gathered_act.reshape(seq_count, seq_len, act_width)
    seq_grads = grad_rot.reshape(seq_count, seq_len, grad_width)
    seq_grad = jnp.einsum("sli,slj->sij", seq_acts, seq_grads, preferred_element_type=jnp.float32)
    scale_seq = lax.rsqrt(seq_lengths.astype(jnp.float32))
    precond = (weights[None, :, :] * seq_grad * scale_seq[:, None, None]).astype(jnp.bfloat16)
    mapped = jnp.einsum("ui,sij->suj", gathered_query, precond, preferred_element_type=jnp.float32)
    per_row = jnp.sum(mapped * query_grad_rot.astype(jnp.float32)[None, :, :], axis=2)
    per_query = jnp.sum(per_row.reshape(seq_count, QUERIES, QUERY_LEN), axis=2)
    partial_scores = per_query.T / math.sqrt(QUERY_LEN * D * FF)
    scores = lax.psum(partial_scores, ("dp", "mp"))
    return (moments, scores)


def solution(mesh):
    return jax.shard_map(
        local,
        mesh=mesh,
        in_specs=(
            P("dp", "mp"),
            P("dp", None),
            P("dp", "mp"),
            P("dp", None),
            P("mp", None),
            P("dp", None),
            P(),
        ),
        out_specs=(P("mp", "dp"), P()),
        check_vma=False,
    )
```

profile of v0, /device:TPU:0, one launch (start us, length us, event | category | flops | bytes accessed | tf_op | source)
XLA Modules:
  0.0 238.3 jit_solution(18068171213799246787)
XLA Ops:
  7.2 0.0 copy-start
  7.2 4.8 %copy.93 = bf16[16,8,8,2048]{3,2,0,1:T(8,128)(2,1)} copy(bf16[16,8,8,2048]{3,2,1,0:T(8,128)(2,1)} %bitcast.72) | data formatting | bytes 8388608 | tf_op jit(solution)/shard_map/all_to_all | solution.py:47
  12.0 0.0 copy-start.2
  12.0 0.0 copy-start.4
  12.0 0.0 copy-start.6
  12.0 5.3 %all-to-all-start = ((bf16[128,8,2048]{2,0,1:T(8,128)(2,1)}), bf16[128,8,2048]{2,0,1:T(8,128)(2,1)}, u32[]{:S(2)}, u32[]{:S(2)}) async-start(bf16[128,8,2048]{2,0,1:T(8,128)(2,1)} %bitcast.68), calls=%async_computation | async-start | bytes 8388608 | tf_op jit(solution)/shard_map/all_to_all | solution.py:47
  17.4 0.0 all-gather.3.cloned.1.call-start
  17.4 0.0 copy-done.2
  17.4 0.0 copy-done.4
  17.4 0.3 fusion.15
  17.8 0.2 copy.44
  18.0 0.0 copy-done.6
  18.0 0.1 select_reduce_fusion
  18.1 0.8 multiply_convert_fusion.4
  18.9 0.0 all-gather.3.cloned.1.call-update
  18.9 4.7 %copy.92 = bf16[16,8,8,2048]{3,2,0,1:T(8,128)(2,1)} copy(bf16[16,8,8,2048]{3,2,1,0:T(8,128)(2,1)} %bitcast.73) | data formatting | bytes 8388608 | tf_op jit(solution)/shard_map/all_to_all | solution.py:48
  23.7 51.3 %all-to-all-done = bf16[128,8,2048]{2,0,1:T(8,128)(2,1)} async-done(((bf16[128,8,2048]{2,0,1:T(8,128)(2,1)}), bf16[128,8,2048]{2,0,1:T(8,128)(2,1)}, u32[]{:S(2)}, u32[]{:S(2)}) %all-to-all-start) | async-done | bytes 4194336 | tf_op jit(solution)/shard_map/all_to_all | solution.py:47
  74.9 0.0 copy-start.3
  74.9 4.7 %all-to-all-start.1 = ((bf16[128,8,2048]{2,0,1:T(8,128)(2,1)}), bf16[128,8,2048]{2,0,1:T(8,128)(2,1)}, u32[]{:S(2)}, u32[]{:S(2)}) async-start(bf16[128,8,2048]{2,0,1:T(8,128)(2,1)} %bitcast.69), calls=%async_computation.1 | async-start | bytes 8388608 | tf_op jit(solution)/shard_map/all_to_all | solution.py:48
  79.6 0.0 all-gather.5.cloned.1.call-start
  79.7 0.0 copy-done.3
  79.7 0.3 convolution_convert_fusion
  80.0 0.9 copy.52
  80.9 0.0 all-gather.5.cloned.1.call-update
  80.9 0.6 reduce_sum.37
  82.2 3.6 %copy.67 = bf16[128,8,16,128]{3,2,1,0:T(8,128)(2,1)S(1)} copy(bf16[128,8,16,128]{3,1,2,0:T(8,128)(2,1)} %bitcast.30) | data formatting | bytes 8388608
  85.8 0.0 copy-done
  85.8 5.9 %multiply_convert_fusion.1 = (bf16[16,128,1024]{2,1,0:T(8,128)(2,1)}, bf16[16,128,1024]{2,1,0:T(8,128)(2,1)}) fusion(bf16[16,128,128]{2,1,0:T(8,128)(2,1)S(1)} %bitcast.63, bf16[1024,16,128]{2,1,0:T(8,128)(2,1)S(1)} %bitcast.65), kind=kOutput, calls=%fused_computation.4 | convolution fusion | flops 545259520 | bytes 13107200 | tf_op jit(solution)/shard_map/nbk,bkc->nbc/dot_general | solution.py:18
  91.8 7.8 %convert_element_type.86 = bf16[4,256,2048]{1,0,2:T(4,128)(2,1)} reshape(bf16[1024,16,128]{0,2,1:T(8,128)(2,1)} %bitcast.66) | data formatting | bytes 8388608 | tf_op jit(solution)/shard_map/convert_element_type | solution.py:50
  99.6 37.5 %all-to-all-done.1 = bf16[128,8,2048]{2,0,1:T(8,128)(2,1)} async-done(((bf16[128,8,2048]{2,0,1:T(8,128)(2,1)}), bf16[128,8,2048]{2,0,1:T(8,128)(2,1)}, u32[]{:S(2)}, u32[]{:S(2)}) %all-to-all-start.1) | async-done | bytes 4194336 | tf_op jit(solution)/shard_map/all_to_all | solution.py:48
  137.1 3.6 %copy.68 = bf16[128,8,16,128]{3,2,1,0:T(8,128)(2,1)S(1)} copy(bf16[128,8,16,128]{3,1,2,0:T(8,128)(2,1)} %bitcast.34) | data formatting | bytes 8388608
  140.7 5.8 %convert_convert_fusion = f32[16,128,1024]{2,1,0:T(8,128)} fusion(bf16[16,128,128]{2,1,0:T(8,128)(2,1)S(1)} %bitcast.64, bf16[1024,16,128]{2,1,0:T(8,128)(2,1)S(1)} %bitcast.67), kind=kOutput, calls=%fused_computation.12 | convolution fusion | flops 541065216 | bytes 13107200 | tf_op jit(solution)/shard_map/nbk,bkc->nbc/dot_general | solution.py:18
  146.5 0.0 all-gather.3.cloned.1.call-done
  146.5 0.0 copy-start.5
  146.5 13.9 %add_divide_fusion = (f32[1024,2048]{1,0:T(8,128)}, f32[1024,2048]{1,0:T(8,128)}) fusion(f32[]{:T(128)S(6)} %convert_element_type.84, bf16[1024,2048]{0,1:T(8,128)(2,1)} %bitcast.71, bf16[1024,1024]{1,0:T(8,128)(2,1)} %all-gather.3.cloned.1.call-done), kind=kOutput, calls=%fused_computation.3 | convolution fusion | flops 4304404480 | bytes 23068676 | tf_op jit(solution)/shard_map/ti,tj->ij/dot_general | solution.py:56
  160.4 0.0 all-gather.5.cloned.1.call-done
  160.4 0.0 copy-done.5
  160.4 0.0 copy-start.1
  160.4 30.5 %fusion = f32[4,1024]{1,0:T(4,128)S(1)} fusion(f32[1024,2048]{0,1:T(8,128)} %bitcast.70, bf16[4,256,1024]{2,1,0:T(8,128)(2,1)S(1)} %bitcast.78, f32[4]{0:T(128)S(1)} %convert_rsqrt_fusion, f32[1024,2048]{1,0:T(8,128)} %get-tuple-element.4, bf16[4,256,2048]{1,0,2:T(4,128)(2,1)} %convert_element_type.86, bf16[1024,1024]{1,0:T(8,128)(2,1)} %all-gather.5.cloned.1.call-done), kind=kOutput, calls=%fused_computation.1 | convolution fusion | flops 21516775424 | bytes 25182224 | tf_op jit(solution)/shard_map/ui,sij->suj/dot_general | solution.py:67
  191.0 0.1 reshape.108
  191.1 0.1 reduce_sum.39
  191.2 40.3 %psum.7 = f32[64,4]{0,1:T(4,128)} all-reduce(f32[64,4]{0,1:T(4,128)S(1)} %multiply_bitcast_fusion), channel_id=1, replica_groups=mesh['dp'=8,'mp'=4] {'dp','mp'}, use_global_device_ids=true, to_apply=%region_4.5 | all-reduce | flops 256 | bytes 2048 | tf_op jit(solution)/shard_map/psum | solution.py:71
  231.5 0.0 copy-done.1
  (4 shorter events, 0.0 us)
Async XLA Ops:
  7.2 78.6 %copy-start = (bf16[2048,128]{1,0:T(8,128)(2,1)S(1)}, bf16[2048,128]{1,0:T(8,128)(2,1)}, u32[]{:S(2)}) copy-start(bf16[2048,128]{1,0:T(8,128)(2,1)} %param.12) | copy-start | bytes 1572868
  12.0 5.4 %copy-start.2 = (bf16[1024,128]{1,0:T(8,128)(2,1)S(1)}, bf16[1024,128]{1,0:T(8,128)(2,1)}, u32[]{:S(2)}) copy-start(bf16[1024,128]{1,0:T(8,128)(2,1)} %param.11) | copy-start | bytes 786436
  12.0 5.4 %copy-start.4 = (bf16[128,1024]{1,0:T(8,128)(2,1)S(1)}, bf16[128,1024]{1,0:T(8,128)(2,1)}, u32[]{:S(2)}) copy-start(bf16[128,1024]{1,0:T(8,128)(2,1)} %param.7) | copy-start | bytes 786436
  12.0 6.0 %copy-start.6 = (s32[4]{0:T(128)S(1)}, s32[4]{0:T(128)}, u32[]{:S(2)}) copy-start(s32[4]{0:T(128)} %param.13) | copy-start | bytes 52
  12.0 62.9 %all-to-all-start = ((bf16[128,8,2048]{2,0,1:T(8,128)(2,1)}), bf16[128,8,2048]{2,0,1:T(8,128)(2,1)}, u32[]{:S(2)}, u32[]{:S(2)}) async-start(bf16[128,8,2048]{2,0,1:T(8,128)(2,1)} %bitcast.68), calls=%async_computation | async-start | bytes 8388608 | tf_op jit(solution)/shard_map/all_to_all | solution.py:47
  17.4 129.2 %all-gather.3.cloned.1.call-start = ((), (), s32[]{:S(2)}) async-start(), calls=%async_computation.2 | async-start | bytes 2359296 | tf_op jit(solution)/shard_map/all_gather | solution.py:43
  74.9 4.8 %copy-start.3 = (bf16[128,1024]{1,0:T(8,128)(2,1)S(1)}, bf16[128,1024]{1,0:T(8,128)(2,1)}, u32[]{:S(2)}) copy-start(bf16[128,1024]{1,0:T(8,128)(2,1)} %param.9) | copy-start | bytes 786436
  74.9 62.2 %all-to-all-start.1 = ((bf16[128,8,2048]{2,0,1:T(8,128)(2,1)}), bf16[128,8,2048]{2,0,1:T(8,128)(2,1)}, u32[]{:S(2)}, u32[]{:S(2)}) async-start(bf16[128,8,2048]{2,0,1:T(8,128)(2,1)} %bitcast.69), calls=%async_computation.1 | async-start | bytes 8388608 | tf_op jit(solution)/shard_map/all_to_all | solution.py:48
  79.6 80.8 %all-gather.5.cloned.1.call-start = ((), (), s32[]{:S(2)}) async-start(), calls=%async_computation.3 | async-start | bytes 2359296 | tf_op jit(solution)/shard_map/all_gather | solution.py:44
  146.5 13.9 %copy-start.5 = (bf16[1024,1024]{1,0:T(8,128)(2,1)S(1)}, bf16[1024,1024]{1,0:T(8,128)(2,1)}, u32[]{:S(2)}) copy-start(bf16[1024,1024]{1,0:T(8,128)(2,1)} %all-gather.3.cloned.1.call-done) | copy-start | bytes 6291460
  160.4 71.1 %copy-start.1 = (bf16[2048,128]{1,0:T(8,128)(2,1)S(1)}, bf16[2048,128]{1,0:T(8,128)(2,1)}, u32[]{:S(2)}) copy-start(bf16[2048,128]{1,0:T(8,128)(2,1)} %param.12) | copy-start | bytes 1572868
Sparse Core Ops, SparseCore 0:
  20.1 49.0 all-gather.2
  82.4 48.9 all-gather.4
where the time goes:
time: 239 us; the launch traced here: 238 us
  waiting for transfers between devices  88.8 us (37%)
  matrix products  56.8 us (24%)
  blocking collectives  40.3 us (17%)
  local copies, waits for them, and re-layouts  25.7 us (11%)
  between operations  14.8 us (6%)
  starting transfers between devices  10.1 us (4%)
    all_to_all x1, waiting for transfers between devices, local(): lax.all_to_all(grad_in, 'dp', split_axis=1, concat_axis=0, tiled=True)  51.3 us
    psum x1, blocking collectives, local(): scores = lax.psum(partial_scores, ('dp', 'mp'))  40.3 us
    all_to_all x1, waiting for transfers between devices, local(): lax.all_to_all(query_grad, 'dp', split_axis=1, concat_axis=0, tiled=True)  37.5 us
    dot_general x1, matrix products, local(): jnp.einsum('ui,sij->suj', gathered_query, precond, preferred_element_type...  30.5 us
    dot_general x1, matrix products, local(): jnp.einsum('ti,tj->ij', act_square, grad_square, preferred_element_type=j...  13.9 us
    dot_general x4, matrix products, rotate(): jnp.einsum('nbk,bkc->nbc', rows_in.reshape(count_rows, blocks, block_size...  12.4 us
    convert_element_type x1, local copies, waits for them, and re-layouts, local(): grad_rot = rotate(grad_cols, grad_basis).astype(jnp.bfloat16)  7.83 us
    unnamed x16, local copies, waits for them, and re-layouts  7.19 us
  transfers between devices with their start and end apart: 4, of which 2 were waited for; matrix products, arithmetic and copies ran while one was open for 20% of the time, Pallas kernels for 0%

commit v1 on v0

--- a/solution.py
+++ b/solution.py
@@ -3,6 +3,7 @@
 import jax.numpy as jnp
 from jax import lax
 from jax.sharding import PartitionSpec as P
+from jax.lax import all_to_all, axis_size
 
 D = 4096
 FF = 16384
@@ -43,9 +44,19 @@
         lax.all_gather(act_rot, "dp", axis=0, tiled=True),
         lax.all_gather(query_act_rot, "dp", axis=0, tiled=True),
     )
+
+    def _process_tables(content):
+        v_next = axis_size("dp")
+        e_now = jnp.split(content, v_next, axis=1)
+        left_arr = jnp.stack(e_now, axis=0)
+        s_next = jnp.concatenate(
+            all_to_all(left_arr, axis_name="dp", split_axis=0, concat_axis=0), axis=0
+        )
+        return s_next
+
     grad_cols, query_cols = (
         lax.all_to_all(grad_in, "dp", split_axis=1, concat_axis=0, tiled=True),
-        lax.all_to_all(query_grad, "dp", split_axis=1, concat_axis=0, tiled=True),
+        _process_tables(query_grad),
     )
     grad_rot = rotate(grad_cols, grad_basis).astype(jnp.bfloat16)
     query_grad_rot = rotate(query_cols, grad_basis).astype(jnp.bfloat16)

time: 239 us -> 241 us (level)
  local copies, waits for them, and re-layouts: 25.7 us -> 36.1 us
  waiting for transfers between devices: 88.8 us -> 79.8 us
    unnamed x16 -> x21, local copies, waits for them, and re-layouts: 7.19 us -> 20.4 us
    all_to_all x1, waiting for transfers between devices: 51.3 us -> 42.2 us  [local(): lax.all_to_all(grad_in, 'dp', split_axis=1, concat_axis=0, tiled=True)]
    all_to_all x1 -> x0, local copies, waits for them, and re-layouts: 4.72 us -> none  [local(): lax.all_to_all(query_grad, 'dp', split_axis=1, concat_axis=0, tiled=True)]
  transfers between devices with their start and end apart: 4 -> 4, of which waited for: 2 -> 2; matrix products, arithmetic and copies ran while one was open for 20% -> 26% of each run, Pallas kernels for 0% -> 0%
where the time goes in v1:
time: 241 us; the launch traced here: 240 us
  waiting for transfers between devices  79.8 us (33%)
  matrix products  58 us (24%)
  blocking collectives  39.3 us (16%)
  local copies, waits for them, and re-layouts  36.1 us (15%)
  between operations  14.8 us (6%)
  starting transfers between devices  9.84 us (4%)
    all_to_all x1, waiting for transfers between devices, local(): lax.all_to_all(grad_in, 'dp', split_axis=1, concat_axis=0, tiled=True)  42.2 us
    psum x1, blocking collectives, local(): scores = lax.psum(partial_scores, ('dp', 'mp'))  39.3 us
    all_to_all x1, waiting for transfers between devices, _process_tables(): all_to_all(left_arr, axis_name='dp', split_axis=0, concat_axis=0)  37.5 us
    dot_general x1, matrix products, local(): jnp.einsum('ui,sij->suj', gathered_query, precond, preferred_element_type...  30.5 us
    unnamed x21, local copies, waits for them, and re-layouts  20.4 us
    dot_general x1, matrix products, local(): jnp.einsum('ti,tj->ij', act_square, grad_square, preferred_element_type=j...  13.9 us
    dot_general x4, matrix products, rotate(): jnp.einsum('nbk,bkc->nbc', rows_in.reshape(count_rows, blocks, block_size...  13.6 us
    convert_element_type x1, local copies, waits for them, and re-layouts, local(): grad_rot = rotate(grad_cols, grad_basis).astype(jnp.bfloat16)  7.82 us
  transfers between devices with their start and end apart: 4, of which 2 were waited for; matrix products, arithmetic and copies ran while one was open for 26% of the time, Pallas kernels for 0%

profile of v1, /device:TPU:0, one launch (start us, length us, event | category | flops | bytes accessed | tf_op | source)
XLA Modules:
  0.0 240.2 jit_solution(787329138706612825)
XLA Ops:
  7.2 0.0 copy-start
  7.2 0.0 all-gather.3.cloned.1.call-start
  7.2 0.8 select_reduce_fusion
  8.0 1.4 fusion.15
  9.4 0.2 copy.42
  9.6 0.8 multiply_convert_fusion.4
  10.4 0.0 all-gather.3.cloned.1.call-update
  10.4 4.8 %copy.87 = bf16[16,8,8,2048]{3,2,0,1:T(8,128)(2,1)} copy(bf16[16,8,8,2048]{3,2,1,0:T(8,128)(2,1)} %bitcast.82) | data formatting | bytes 8388608 | tf_op jit(solution)/shard_map/all_to_all | solution.py:58
  15.2 5.2 %all-to-all-start = ((bf16[128,8,2048]{2,0,1:T(8,128)(2,1)}), bf16[128,8,2048]{2,0,1:T(8,128)(2,1)}, u32[]{:S(2)}, u32[]{:S(2)}) async-start(bf16[128,8,2048]{2,0,1:T(8,128)(2,1)} %bitcast.79), calls=%async_computation | async-start | bytes 8388608 | tf_op jit(solution)/shard_map/all_to_all | solution.py:58
  20.4 1.9 bitcast_dynamic-update-slice_fusion.7
  22.4 1.9 bitcast_dynamic-update-slice_fusion.6
  24.3 1.9 bitcast_dynamic-update-slice_fusion.5
  26.2 1.9 bitcast_dynamic-update-slice_fusion.4
  28.0 1.9 bitcast_dynamic-update-slice_fusion.3
  29.9 1.9 bitcast_dynamic-update-slice_fusion.2
  31.8 1.9 bitcast_dynamic-update-slice_fusion.1
  33.7 1.9 bitcast_dynamic-update-slice_fusion
  35.6 0.0 copy-start.2
  35.6 0.0 copy-start.3
  35.6 0.0 copy-start.5
  35.6 42.2 %all-to-all-done = bf16[128,8,2048]{2,0,1:T(8,128)(2,1)} async-done(((bf16[128,8,2048]{2,0,1:T(8,128)(2,1)}), bf16[128,8,2048]{2,0,1:T(8,128)(2,1)}, u32[]{:S(2)}, u32[]{:S(2)}) %all-to-all-start) | async-done | bytes 4194336 | tf_op jit(solution)/shard_map/all_to_all | solution.py:58
  77.8 4.6 %all-to-all-start.1 = ((bf16[8,128,2048]{2,1,0:T(8,128)(2,1)}), bf16[8,128,2048]{2,1,0:T(8,128)(2,1)}, u32[]{:S(2)}, u32[]{:S(2)}) async-start(bf16[8,128,2048]{2,1,0:T(8,128)(2,1)} %bitcast_dynamic-update-slice_fusion), calls=%async_computation.1 | async-start | bytes 8388608 | tf_op jit(solution)/shard_map/all_to_all | solution.py:53
  82.4 0.0 all-gather.5.cloned.1.call-start
  82.4 0.0 copy-done.2
  82.4 0.0 copy-done.3
  82.4 0.3 convolution_convert_fusion
  82.8 0.9 copy.50
  83.6 0.0 all-gather.5.cloned.1.call-update
  83.6 0.0 copy-done.5
  83.7 0.6 reduce_sum.37
  85.0 3.6 %copy.63 = bf16[128,8,16,128]{3,2,1,0:T(8,128)(2,1)S(1)} copy(bf16[128,8,16,128]{3,1,2,0:T(8,128)(2,1)} %bitcast.35) | data formatting | bytes 8388608
  88.5 0.0 copy-done
  88.5 5.9 %multiply_convert_fusion.1 = (bf16[16,128,1024]{2,1,0:T(8,128)(2,1)}, bf16[16,128,1024]{2,1,0:T(8,128)(2,1)}) fusion(bf16[16,128,128]{2,1,0:T(8,128)(2,1)S(1)} %bitcast.74, bf16[1024,16,128]{2,1,0:T(8,128)(2,1)S(1)} %bitcast.76), kind=kOutput, calls=%fused_computation.4 | convolution fusion | flops 545259520 | bytes 13107200 | tf_op jit(solution)/shard_map/nbk,bkc->nbc/dot_general | solution.py:19
  94.5 7.8 %convert_element_type.86 = bf16[4,256,2048]{1,0,2:T(4,128)(2,1)} reshape(bf16[1024,16,128]{0,2,1:T(8,128)(2,1)} %bitcast.77) | data formatting | bytes 8388608 | tf_op jit(solution)/shard_map/convert_element_type | solution.py:61
  102.3 37.5 %all-to-all-done.1 = bf16[8,128,2048]{2,1,0:T(8,128)(2,1)} async-done(((bf16[8,128,2048]{2,1,0:T(8,128)(2,1)}), bf16[8,128,2048]{2,1,0:T(8,128)(2,1)}, u32[]{:S(2)}, u32[]{:S(2)}) %all-to-all-start.1) | async-done | bytes 4194336 | tf_op jit(solution)/shard_map/all_to_all | solution.py:53
  139.8 3.6 %copy.64 = bf16[128,8,16,128]{3,2,1,0:T(8,128)(2,1)S(1)} copy(bf16[128,8,16,128]{3,1,2,0:T(8,128)(2,1)} %bitcast.39) | data formatting | bytes 8388608
  143.4 5.9 %convert_convert_fusion = f32[16,1024,128]{1,2,0:T(8,128)} fusion(bf16[16,128,128]{2,1,0:T(8,128)(2,1)S(1)} %bitcast.75, bf16[1024,16,128]{2,1,0:T(8,128)(2,1)S(1)} %bitcast.78), kind=kOutput, calls=%fused_computation.11 | convolution fusion | flops 541065216 | bytes 13107200 | tf_op jit(solution)/shard_map/nbk,bkc->nbc/dot_general | solution.py:19
  149.4 0.0 all-gather.3.cloned.1.call-done
  149.4 0.0 copy-start.4
  149.4 13.9 %add_divide_fusion = (f32[1024,2048]{1,0:T(8,128)}, f32[1024,2048]{1,0:T(8,128)}) fusion(f32[]{:T(128)S(6)} %convert_element_type.84, bf16[1024,2048]{0,1:T(8,128)(2,1)} %bitcast.81, bf16[1024,1024]{1,0:T(8,128)(2,1)} %all-gather.3.cloned.1.call-done), kind=kOutput, calls=%fused_computation.3 | convolution fusion | flops 4304404480 | bytes 23068676 | tf_op jit(solution)/shard_map/ti,tj->ij/dot_general | solution.py:67
  163.3 0.0 all-gather.5.cloned.1.call-done
  163.3 0.0 copy-done.4
  163.3 0.0 copy-start.1
  163.3 30.5 %fusion = f32[4,1024]{1,0:T(4,128)S(1)} fusion(f32[1024,2048]{0,1:T(8,128)} %bitcast.80, bf16[4,256,1024]{2,1,0:T(8,128)(2,1)S(1)} %bitcast.87, f32[4]{0:T(128)S(1)} %convert_rsqrt_fusion, f32[1024,2048]{1,0:T(8,128)} %get-tuple-element.4, bf16[4,256,2048]{1,0,2:T(4,128)(2,1)} %convert_element_type.86, bf16[1024,1024]{1,0:T(8,128)(2,1)} %all-gather.5.cloned.1.call-done), kind=kOutput, calls=%fused_computation.1 | convolution fusion | flops 21516775424 | bytes 25182224 | tf_op jit(solution)/shard_map/ui,sij->suj/dot_general | solution.py:78
  193.8 0.1 reshape.100
  193.9 0.1 reduce_sum.39
  194.1 39.3 %psum.7 = f32[64,4]{0,1:T(4,128)} all-reduce(f32[64,4]{0,1:T(4,128)S(1)} %multiply_bitcast_fusion), channel_id=1, replica_groups=mesh['dp'=8,'mp'=4] {'dp','mp'}, use_global_device_ids=true, to_apply=%region_4.5 | all-reduce | flops 256 | bytes 2048 | tf_op jit(solution)/shard_map/psum | solution.py:82
  233.4 0.0 copy-done.1
  (4 shorter events, 0.0 us)
Async XLA Ops:
  7.2 81.4 %copy-start = (bf16[2048,128]{1,0:T(8,128)(2,1)S(1)}, bf16[2048,128]{1,0:T(8,128)(2,1)}, u32[]{:S(2)}) copy-start(bf16[2048,128]{1,0:T(8,128)(2,1)} %param.12) | copy-start | bytes 1572868
  7.2 142.2 %all-gather.3.cloned.1.call-start = ((), (), s32[]{:S(2)}) async-start(), calls=%async_computation.2 | async-start | bytes 2359296 | tf_op jit(solution)/shard_map/all_gather | solution.py:44
  15.2 62.6 %all-to-all-start = ((bf16[128,8,2048]{2,0,1:T(8,128)(2,1)}), bf16[128,8,2048]{2,0,1:T(8,128)(2,1)}, u32[]{:S(2)}, u32[]{:S(2)}) async-start(bf16[128,8,2048]{2,0,1:T(8,128)(2,1)} %bitcast.79), calls=%async_computation | async-start | bytes 8388608 | tf_op jit(solution)/shard_map/all_to_all | solution.py:58
  35.6 46.9 %copy-start.2 = (bf16[1024,128]{1,0:T(8,128)(2,1)S(1)}, bf16[1024,128]{1,0:T(8,128)(2,1)}, u32[]{:S(2)}) copy-start(bf16[1024,128]{1,0:T(8,128)(2,1)} %param.11) | copy-start | bytes 786436
  35.6 46.9 %copy-start.3 = (bf16[128,1024]{1,0:T(8,128)(2,1)S(1)}, bf16[128,1024]{1,0:T(8,128)(2,1)}, u32[]{:S(2)}) copy-start(bf16[128,1024]{1,0:T(8,128)(2,1)} %param.9) | copy-start | bytes 786436
  35.6 48.1 %copy-start.5 = (s32[4]{0:T(128)S(1)}, s32[4]{0:T(128)}, u32[]{:S(2)}) copy-start(s32[4]{0:T(128)} %param.13) | copy-start | bytes 52
  77.8 62.0 %all-to-all-start.1 = ((bf16[8,128,2048]{2,1,0:T(8,128)(2,1)}), bf16[8,128,2048]{2,1,0:T(8,128)(2,1)}, u32[]{:S(2)}, u32[]{:S(2)}) async-start(bf16[8,128,2048]{2,1,0:T(8,128)(2,1)} %bitcast_dynamic-update-slice_fusion), calls=%async_computation.1 | async-start | bytes 8388608 | tf_op jit(solution)/shard_map/all_to_all | solution.py:53
  82.4 80.9 %all-gather.5.cloned.1.call-start = ((), (), s32[]{:S(2)}) async-start(), calls=%async_computation.3 | async-start | bytes 2359296 | tf_op jit(solution)/shard_map/all_gather | solution.py:45
  149.4 13.9 %copy-start.4 = (bf16[1024,1024]{1,0:T(8,128)(2,1)S(1)}, bf16[1024,1024]{1,0:T(8,128)(2,1)}, u32[]{:S(2)}) copy-start(bf16[1024,1024]{1,0:T(8,128)(2,1)} %all-gather.3.cloned.1.call-done) | copy-start | bytes 6291460
  163.3 70.1 %copy-start.1 = (bf16[2048,128]{1,0:T(8,128)(2,1)S(1)}, bf16[2048,128]{1,0:T(8,128)(2,1)}, u32[]{:S(2)}) copy-start(bf16[2048,128]{1,0:T(8,128)(2,1)} %param.12) | copy-start | bytes 1572868
Sparse Core Ops, SparseCore 0:
  10.6 51.8 all-gather.2
  85.1 47.9 all-gather.4
